TPU v7x, 512 devices: a whole 4x8x8 slice. The times are simulated.
512 devices in a mesh: slab: 64 (over x, y, z_lo), grp: 8 (over z_hi, core).
Axes of the slice: x: 4, y: 8, z: 8 (z_hi: 4, z_lo: 2; z = z_hi * 2 + z_lo), core: 2. Of those that a mesh axis runs over, the one named last changes fastest.
Arguments:
- echo_data: bfloat16 [64, 1024, 2048], P('slab', 'grp'), may hold values from -6 to 6
- acquirer: int32 [3], replicated, may hold values from 0 to 63, as said below
- panels: bfloat16 [64, 3, 64, 128, 128], P('slab', None, 'grp'), may hold values from -0.00390625 to 0.00390625
- block_count: int32 [64, 3], P('slab'), may hold values from 16 to 64, as said below
- block_rows: int32 [64, 3, 64], P('slab'), may hold values from 0 to 7
- block_columns: int32 [64, 3, 64], P('slab'), may hold values from 0 to 15
- apodization: float32 [16, 1024], P(None, 'grp'), may hold values from 0.25 to 2.5
- window_index: int32 [65536], P('slab'), may hold values from 0 to 15
Outputs:
- image: float32 [65536], P(('slab', 'grp'))
Inputs may be any that keep to these rules, and one draw needn't show every extreme that they name: `acquirer`: 3 distinct slab indices, the last slab index always among them. `block_count`: slots below the count are live, the others unused; some slab and transmit has all 64 live in every draw.
All inputs are finite; a program needn't handle non-finite values.
Results may differ from a plain program's by a relative error of at most 0.0003.
Values may be sent and summed in bfloat16 or wider, within the bound.
No kernel may reach another device: no remote copies, remote signals or barrier semaphores. Data moves between devices by JAX's collectives and lax.ppermute only.
A program may use at most 128 MiB of HBM per device.

v0:
```python
import math
import jax
import jax.numpy as jnp
from jax import lax
from jax.sharding import PartitionSpec as P


def from_root(block, axis, holder):
    block = jnp.where(lax.axis_index(axis) == holder, block, jnp.zeros_like(block))
    return lax.psum(block, axis)


def table_rows(window_index, table):
    windows = table.shape[0]
    onehot = (window_index[:, None] == jnp.arange(windows, dtype=jnp.int32)[None, :]).astype(
        jnp.float32
    )
    return jnp.dot(
        onehot, table, precision=lax.Precision.HIGHEST, preferred_element_type=jnp.float32
    )


def block_terms(piece, columns, signal):
    block_size = piece.shape[-1]
    channels = signal.shape[0]
    grid = signal.reshape(channels, signal.shape[1] // block_size, block_size)
    picked = jnp.take(grid, columns, axis=1)
    return jnp.einsum("kvs,cks->kvc", piece, picked, preferred_element_type=jnp.float32)


def place_rows(terms, rows, live, row_blocks):
    onehot = (rows[:, None] == jnp.arange(row_blocks, dtype=jnp.int32)[None, :]).astype(
        jnp.float32
    ) * live[:, None]
    return jnp.einsum("kr,kvc->rvc", onehot, terms, precision=lax.Precision.HIGHEST)


def masked_slots(running, piece, rows, columns, live, signal):
    width = piece.shape[0]
    block_size = piece.shape[-1]
    channels = signal.shape[0]
    limit = max(1, (1 << 18) // (block_size * channels))
    group = math.gcd(width, limit)
    turns = width // group
    grouped = (
        piece.reshape(turns, group, block_size, block_size),
        rows.reshape(turns, group),
        columns.reshape(turns, group),
        live.reshape(turns, group),
    )

    def one_group(current, inputs):
        group_piece, group_rows, group_columns, group_live = inputs
        terms = block_terms(group_piece, group_columns, signal)
        return (current + place_rows(terms, group_rows, group_live, current.shape[0]), None)

    result, unused = lax.scan(one_group, running, grouped)
    return result


def add_slots(running, piece, rows_all, columns_all, count, signal):
    width = piece.shape[0]
    live = (jnp.arange(width, dtype=jnp.int32) < count).astype(jnp.float32)
    return masked_slots(running, piece, rows_all, columns_all, live, signal)


def per_device(
    echo_data, acquirer, panels, block_count, block_rows, block_columns, apodization, window_index
):
    signal_own = echo_data[0]
    block_size = panels.shape[-1]
    voxel_count = window_index.shape[0]
    row_blocks = voxel_count // block_size
    weights = table_rows(window_index, apodization)
    running = jnp.zeros((row_blocks, block_size, signal_own.shape[0]), jnp.float32)
    for transmit in range(acquirer.shape[0]):
        signal = from_root(signal_own, "slab", acquirer[transmit])
        rows_all = block_rows[0, transmit]
        columns_all = block_columns[0, transmit]
        count = block_count[0, transmit]

        def fold_panels(
            current,
            piece,
            start,
            signal=signal,
            rows_all=rows_all,
            columns_all=columns_all,
            count=count,
        ):
            return add_slots(current, piece, rows_all, columns_all, count, signal)

        running = fold_panels(
            running, lax.all_gather(panels[0, transmit], "grp", axis=0, tiled=True), jnp.int32(0)
        )
    partial_value = jnp.sum(running.reshape(voxel_count, running.shape[2]) * weights, axis=1)
    return lax.psum_scatter(partial_value, "grp", scatter_dimension=0, tiled=True)


def solution(mesh):
    return jax.shard_map(
        per_device,
        mesh=mesh,
        in_specs=(
            P("slab", "grp", None),
            P(),
            P("slab", None, "grp", None, None),
            P("slab", None),
            P("slab", None, None),
            P("slab", None, None),
            P(None, "grp"),
            P("slab"),
        ),
        out_specs=P(("slab", "grp")),
        check_vma=False,
    )
```

profile of v0, /device:TPU:1, one launch (start us, length us, event | category | flops | bytes accessed | tf_op | source)
XLA Modules:
  0.0 722.1 jit_solution(10459350146008842801)
XLA Ops:
  7.4 1.4 fusion.66
  20.4 580.0 %all-reduce.4.cloned.1.call-done = (bf16[128,2048]{0,1:T(8,128)(2,1)}, bf16[128,2048]{0,1:T(8,128)(2,1)}, bf16[128,2048]{0,1:T(8,128)(2,1)}) async-done(((bf16[128,2048]{0,1:T(8,128)(2,1)}, bf16[128,2048]{0,1:T(8,128)(2,1)}, bf16[128,2048]{0,1:T(8,128)(2,1)}), (bf16[128,2048]{0,1:T(8,128)(2,1)}, bf16[128,2048]{0,1:T(8,128)(2,1)}, bf16[128,2048]{0,1:T(8,128)(2,1)})) %all-reduce.4.cloned.1.call-update) | async-done | bytes 1572880 | tf_op jit(solution)/shard_map/psum | solution.py:10
  600.5 20.0 %while.33 = (s32[]{:T(128)}, f32[8,128,128]{2,0,1:T(8,128)S(1)}, s32[4,16]{1,0:T(4,128)S(1)}, f32[4,16]{1,0:T(4,128)S(1)}, bf16[4,16,128,128]{3,2,1,0:T(8,128)(2...) while((s32[]{:T(128)}, f32[8,128,128]{2,0,1:T(8,128)S(1)}, ...), condition=%wide.region_2.4_spmd.clone, body=%wide.region_1.3_spmd.clone.sunk | while | flops 92800352 | bytes 6296851 | solution.py:57
  600.5 1.4 copy.56
  602.5 1.6 fusion.107
  607.5 1.6 fusion.107
  612.5 1.6 fusion.107
  617.5 1.6 fusion.107
  620.5 15.9 %while.31 = (s32[]{:T(128)}, f32[8,128,128]{2,0,1:T(8,128)S(1)}, s32[4,16]{1,0:T(4,128)S(1)}, f32[4,16]{1,0:T(4,128)S(1)}, bf16[4,16,128,128]{3,2,1,0:T(8,128)(2...) while((s32[]{:T(128)}, f32[8,128,128]{2,0,1:T(8,128)S(1)}, s32[4,16]{1,0:T(4,128)S(1)}, ...), condition=%wide.region_5.7_spmd, body=%wide.region_4.6_spmd.sunk | while | flops 92669280 | bytes 6296833 | solution.py:57
  621.5 1.6 fusion.93
  623.2 1.3 convolution_add_fusion.6
  625.5 1.6 fusion.93
  627.2 1.3 convolution_add_fusion.6
  629.5 1.6 fusion.93
  631.1 1.3 convolution_add_fusion.6
  633.5 1.6 fusion.93
  636.5 15.9 %while.32 = (s32[]{:T(128)}, f32[8,128,128]{2,0,1:T(8,128)S(1)}, s32[4,16]{1,0:T(4,128)S(1)}, f32[4,16]{1,0:T(4,128)S(1)}, bf16[4,16,128,128]{3,2,1,0:T(8,128)(2...) while((s32[]{:T(128)}, f32[8,128,128]{2,0,1:T(8,128)S(1)}, ...), condition=%wide.region_8.10_spmd, body=%wide.region_7.9_spmd.sunk | while | flops 92669280 | bytes 6296833 | solution.py:57
  637.5 1.6 fusion.100
  641.5 1.6 fusion.100
  643.2 1.3 convolution_add_fusion.7
  645.5 1.6 fusion.100
  649.5 1.6 fusion.100
  651.1 1.3 convolution_add_fusion.7
  653.4 60.5 %all-reduce = f32[1024]{0:T(1024)S(1)} all-reduce(f32[1024]{0:T(1024)S(1)} %fusion.57), channel_id=5, replica_groups=mesh['slab'=64,'grp'=8] {'grp'}, use_global_device_ids=true, to_apply=%region_10.12.clone | all-reduce | flops 1024 | bytes 8192
  (124 shorter events, 34.4 us)
Async XLA Ops:
  7.4 645.4 %copy-start = (f32[16,128]{1,0:T(8,128)S(1)}, f32[16,128]{1,0:T(8,128)}, u32[]{:S(2)}) copy-start(f32[16,128]{1,0:T(8,128)} %param.22) | copy-start | bytes 24580
  7.4 593.1 %all-reduce.4.cloned.1.call-start = ((), (), s32[]{:S(2)}) async-start(), calls=%async_computation.3 | async-start | bytes 3145728 | tf_op jit(solution)/shard_map/psum | solution.py:10
  12.0 1.6 copy-start.3
  13.2 2.4 copy-start.6
  13.2 2.4 copy-start.7
  13.2 2.6 copy-start.4
  13.2 587.2 %all-gather.7.cloned.1.call-start = ((), (), s32[]{:S(2)}) async-start(), calls=%async_computation | async-start | bytes 2359296 | tf_op jit(solution)/shard_map/all_gather | solution.py:94
  14.4 606.1 %all-gather.9.cloned.1.call-start = ((), (), s32[]{:S(2)}) async-start(), calls=%async_computation.1 | async-start | bytes 2359296 | tf_op jit(solution)/shard_map/all_gather | solution.py:94
  15.0 621.5 %all-gather.11.cloned.1.call-start = ((), (), s32[]{:S(2)}) async-start(), calls=%async_computation.2 | async-start | bytes 2359296 | tf_op jit(solution)/shard_map/all_gather | solution.py:94
  600.5 20.0 %copy-start.2 = (bf16[128,2048]{0,1:T(8,128)(2,1)S(1)}, bf16[128,2048]{0,1:T(8,128)(2,1)}, u32[]{:S(2)}) copy-start(bf16[128,2048]{0,1:T(8,128)(2,1)} %get-tuple-element.389) | copy-start | bytes 1572868
  620.5 16.0 %copy-start.1 = (bf16[128,2048]{0,1:T(8,128)(2,1)S(1)}, bf16[128,2048]{0,1:T(8,128)(2,1)}, u32[]{:S(2)}) copy-start(bf16[128,2048]{0,1:T(8,128)(2,1)} %get-tuple-element.413) | copy-start | bytes 1572868
  636.5 16.3 %copy-start.5 = (s32[1024]{0:T(1024)S(1)}, s32[1024]{0:T(1024)}, u32[]{:S(2)}) copy-start(s32[1024]{0:T(1024)} %param.23) | copy-start | bytes 12292
Sparse Core Ops, SparseCore 0:
  13.4 587.0 all-reduce.3
Sparse Core Ops, SparseCore 1:
  15.9 46.7 all-gather.6
  64.8 39.5 all-gather.8
  106.6 39.3 all-gather.10
where the time goes:
time: 723 us; the launch traced here: 722 us
  waiting for transfers between devices  581 us (80%)
  blocking collectives  60.5 us (8%)
  matrix products  35.8 us (5%)
  local copies, waits for them, and re-layouts  22.7 us (3%)
  between operations  17.7 us (2%)
    psum x1, waiting for transfers between devices, from_root(): return lax.psum(block, axis)  580 us
    unnamed x1, blocking collectives  60.5 us
    dot_general x12, matrix products, block_terms(): jnp.einsum('kvs,cks->kvc', piece, picked, preferred_element_type=jnp.floa...  19.3 us
    dot_general x12, matrix products, place_rows(): jnp.einsum('kr,kvc->rvc', onehot, terms, precision=lax.Precision.HIGHEST)  15.9 us
  transfers between devices with their start and end apart: 4, of which 1 were waited for; matrix products, arithmetic and copies ran while one was open for 6% of the time, Pallas kernels for 0%

commit v1 on v0

--- a/solution.py
+++ b/solution.py
@@ -5,9 +5,14 @@
 from jax.sharding import PartitionSpec as P
 
 
+def _register_case(shard_in, chip_axis):
+    r2 = lax.all_gather(shard_in, chip_axis).sum(axis=0)
+    return r2
+
+
 def from_root(block, axis, holder):
     block = jnp.where(lax.axis_index(axis) == holder, block, jnp.zeros_like(block))
-    return lax.psum(block, axis)
+    return _register_case(block, axis)
 
 
 def table_rows(window_index, table):

time: 723 us -> 2370 us (3.28)
  waiting for transfers between devices: 581 us -> 2240 us
  blocking collectives: 60.5 us -> 13.9 us
  other arithmetic: 3.25 us -> 38.3 us
    all_gather x0 -> x3, waiting for transfers between devices: none -> 2150 us  [_register_case(): r2 = lax.all_gather(shard_in, chip_axis).sum(axis=0)]
    psum x1 -> x0, waiting for transfers between devices: 580 us -> none  [from_root(): return lax.psum(block, axis)]
    all_gather x3, waiting for transfers between devices: 0.05 us -> 86.7 us  [per_device(): lax.all_gather(panels[0, transmit], 'grp', axis=0, tiled=True)]
    unnamed x1, blocking collectives: 60.5 us -> 13.9 us
    reduce_sum x0 -> x3, other arithmetic: none -> 34 us  [_register_case(): r2 = lax.all_gather(shard_in, chip_axis).sum(axis=0)]
  transfers between devices with their start and end apart: 4 -> 6, of which waited for: 1 -> 6; matrix products, arithmetic and copies ran while one was open for 6% -> 3% of each run, Pallas kernels for 0% -> 0%
where the time goes in v1:
time: 2370 us; the launch traced here: 2360 us
  waiting for transfers between devices  2240 us (95%)
  other arithmetic  38.3 us (2%)
  matrix products  35.9 us (2%)
    all_gather x3, waiting for transfers between devices, _register_case(): r2 = lax.all_gather(shard_in, chip_axis).sum(axis=0)  2150 us
    all_gather x3, waiting for transfers between devices, per_device(): lax.all_gather(panels[0, transmit], 'grp', axis=0, tiled=True)  86.7 us
  transfers between devices with their start and end apart: 6, of which 6 were waited for; matrix products, arithmetic and copies ran while one was open for 3% of the time, Pallas kernels for 0%

profile of v1, /device:TPU:1, one launch (start us, length us, event | category | flops | bytes accessed | tf_op | source)
XLA Modules:
  0.0 2364.7 jit_solution(10899181896365958502)
XLA Ops:
  9.8 2.2 broadcast_select_fusion
  20.4 724.3 %all-gather.10.cloned.1.call-done = bf16[64,128,2048]{2,1,0:T(8,128)(2,1)} async-done(((bf16[1,128,2048]{2,1,0:T(8,128)(2,1)}), bf16[64,128,2048]{2,1,0:T(8,128)(2,1)}) %all-gather.10.cloned.1.call-update) | async-done | bytes 33554448 | tf_op jit(solution)/shard_map/all_gather | solution.py:9
  744.7 11.3 reduce_sum.45
  756.3 31.6 %all-gather.16.cloned.1.call-done = bf16[1,1,64,128,128]{4,3,1,0,2:T(8,128)(2,1)} async-done(((bf16[1,1,8,128,128]{4,3,1,0,2:T(8,128)(2,1)}), bf16[1,1,64,128,128]{4,3,1,0,2:T(8,128)(2,1)}) %all-gather.16.cloned.1.call-update) | async-done | bytes 2097168 | tf_op jit(solution)/shard_map/all_gather | solution.py:99
  787.9 15.9 while.33
  788.9 1.6 fusion.107
  792.9 1.6 fusion.107
  796.9 1.6 fusion.107
  800.8 1.7 fusion.107
  803.9 710.4 %all-gather.12.cloned.1.call-done = bf16[64,128,2048]{2,1,0:T(8,128)(2,1)} async-done(((bf16[1,128,2048]{2,1,0:T(8,128)(2,1)}), bf16[64,128,2048]{2,1,0:T(8,128)(2,1)}) %all-gather.12.cloned.1.call-update) | async-done | bytes 33554448 | tf_op jit(solution)/shard_map/all_gather | solution.py:9
  1514.2 11.3 reduce_sum.46
  1525.9 718.0 %all-gather.14.cloned.1.call-done = bf16[64,128,2048]{2,1,0:T(8,128)(2,1)} async-done(((bf16[1,128,2048]{2,1,0:T(8,128)(2,1)}), bf16[64,128,2048]{2,1,0:T(8,128)(2,1)}) %all-gather.14.cloned.1.call-update) | async-done | bytes 33554448 | tf_op jit(solution)/shard_map/all_gather | solution.py:9
  2243.8 11.3 reduce_sum.47
  2255.5 31.4 %all-gather.18.cloned.1.call-done = bf16[1,1,64,128,128]{4,3,1,0,2:T(8,128)(2,1)} async-done(((bf16[1,1,8,128,128]{4,3,1,0,2:T(8,128)(2,1)}), bf16[1,1,64,128,128]{4,3,1,0,2:T(8,128)(2,1)}) %all-gather.18.cloned.1.call-update) | async-done | bytes 2097168 | tf_op jit(solution)/shard_map/all_gather | solution.py:99
  2286.9 15.9 while.31
  2291.9 1.6 fusion.93
  2295.9 1.6 fusion.93
  2299.9 1.6 fusion.93
  2302.9 23.7 %all-gather.20.cloned.1.call-done = bf16[1,1,64,128,128]{4,3,1,0,2:T(8,128)(2,1)} async-done(((bf16[1,1,8,128,128]{4,3,1,0,2:T(8,128)(2,1)}), bf16[1,1,64,128,128]{4,3,1,0,2:T(8,128)(2,1)}) %all-gather.20.cloned.1.call-update) | async-done | bytes 2097168 | tf_op jit(solution)/shard_map/all_gather | solution.py:99
  2326.6 15.9 while.32
  2327.5 1.6 fusion.100
  2331.5 1.6 fusion.100
  2339.5 1.6 fusion.100
  2343.4 13.9 all-reduce
  (131 shorter events, 42.3 us)
Async XLA Ops:
  6.5 2336.2 %copy-start = (f32[16,128]{1,0:T(8,128)S(1)}, f32[16,128]{1,0:T(8,128)}, u32[]{:S(2)}) copy-start(f32[16,128]{1,0:T(8,128)} %param.22) | copy-start | bytes 24580
  6.5 5.6 copy-start.1
  6.5 738.2 %all-gather.10.cloned.1.call-start = ((), (), s32[]{:S(2)}) async-start(), calls=%async_computation | async-start | bytes 34078720 | tf_op jit(solution)/shard_map/all_gather | solution.py:9
  12.0 3.6 copy-start.4
  12.0 3.6 copy-start.5
  12.0 3.8 copy-start.2
  12.1 775.8 %all-gather.16.cloned.1.call-start = ((), (), s32[]{:S(2)}) async-start(), calls=%async_computation.3 | async-start | bytes 2359296 | tf_op jit(solution)/shard_map/all_gather | solution.py:99
  13.1 1501.1 %all-gather.12.cloned.1.call-start = ((), (), s32[]{:S(2)}) async-start(), calls=%async_computation.1 | async-start | bytes 34078720 | tf_op jit(solution)/shard_map/all_gather | solution.py:9
  13.8 2230.0 %all-gather.14.cloned.1.call-start = ((), (), s32[]{:S(2)}) async-start(), calls=%async_computation.2 | async-start | bytes 34078720 | tf_op jit(solution)/shard_map/all_gather | solution.py:9
  14.4 2272.5 %all-gather.18.cloned.1.call-start = ((), (), s32[]{:S(2)}) async-start(), calls=%async_computation.4 | async-start | bytes 2359296 | tf_op jit(solution)/shard_map/all_gather | solution.py:99
  15.0 2311.6 %all-gather.20.cloned.1.call-start = ((), (), s32[]{:S(2)}) async-start(), calls=%async_computation.5 | async-start | bytes 2359296 | tf_op jit(solution)/shard_map/all_gather | solution.py:99
  2326.6 16.2 copy-start.3
Sparse Core Ops, SparseCore 0:
  12.2 732.4 all-gather.9
  746.9 41.0 all-gather.15
  790.0 724.1 all-gather.11
  1516.2 727.6 all-gather.13
  2245.8 41.0 all-gather.17
  2288.9 37.5 all-gather.19
